TPU v7x, 256 devices: a whole 4x4x8 slice. The times are simulated.
256 devices in a mesh: row: 16 (over y, z_lo), col: 8 (over x, core), tp: 2 (over z_hi).
Axes of the slice: x: 4, y: 4, z: 8 (z_hi: 2, z_lo: 4; z = z_hi * 4 + z_lo), core: 2. Of those that a mesh axis runs over, the one named last changes fastest.
Arguments:
- gram: float32 [8, 16, 128, 1, 8, 2048], P(None, 'row', 'tp', None, 'col'), may hold values from -24 to 24
- inv_factor: bfloat16 [1024, 1024], replicated, as said below
- cross_gram: bfloat16 [8, 16, 128, 1024], P(None, 'row', 'tp'), may hold values from -24 to 24
- down_rows: bfloat16 [29568, 4096], P(('row', 'tp'), 'col'), may hold values from -0.03125 to 0.03125
- removed: int32 [1024], replicated, may hold values from 0 to 29567, as said below
Outputs:
- updated: float32 [8, 16, 128, 1, 8, 2048], P(None, 'row', 'tp', None, 'col')
- rhs_next: float32 [8, 16, 128, 4096], P(None, 'row', 'tp', 'col')
Inputs may be any that keep to these rules, and one draw needn't show every extreme that they name: `inv_factor`: zero above the diagonal. `removed`: distinct ids in ascending order; among the neurons s * 924 to (s + 1) * 924 - 1 of any shard s at most 128 are listed, and one shard holds exactly 128.
All inputs are finite; a program needn't handle non-finite values.
Results may differ from a plain program's by a relative error of at most 0.0003.
Values may be sent and summed in bfloat16 or wider, within the bound.
A program may use at most 128 MiB of HBM per device.

v0:
```python
import jax
import jax.numpy as jnp
from jax import lax
from jax.sharding import PartitionSpec as P


def broadcast(block, axis, holder):
    block = jnp.where(lax.axis_index(axis) == holder, block, jnp.zeros_like(block))
    return lax.psum(block, axis)


def per_device(gram, inv_factor, cross_gram, down_rows, removed):
    highest = lax.Precision.HIGHEST
    cycles = gram.shape[0]
    half = gram.shape[2]
    col_cycles = gram.shape[3]
    block = gram.shape[5]
    rows_local = cycles * half
    panel_width = inv_factor.shape[0]
    grid = gram.reshape(rows_local, col_cycles, block)
    factor = inv_factor.astype(jnp.float32)
    head_columns = grid[:, 0, :panel_width]
    panel = broadcast(head_columns, "col", 0)
    left = jnp.dot(panel, factor.T, precision=highest, preferred_element_type=jnp.float32)
    col_count = lax.axis_size("col")
    by_cycle = left.reshape(col_cycles, col_count, half, panel_width)
    wanted = lax.dynamic_index_in_dim(by_cycle, lax.axis_index("col"), axis=1, keepdims=False)
    product = jnp.einsum(
        "rp,cwp->rcw",
        left,
        lax.all_gather(wanted, ("row", "tp"), axis=1, tiled=True),
        precision=highest,
        preferred_element_type=jnp.float32,
    )
    updated = grid - product
    shard = down_rows.shape[0]
    count_all = removed.shape[0]
    member = lax.axis_index(("row", "tp"))
    owner = removed // shard
    capacity = 4 * count_all // lax.axis_size(("row", "tp"))
    earlier = jnp.sum(owner[None, :] < owner[:, None], axis=1)
    within = jnp.arange(count_all, dtype=jnp.int32) - earlier
    own_start = jnp.sum(owner < member)
    slot_ids = jnp.clip(own_start + jnp.arange(capacity, dtype=jnp.int32), 0, count_all - 1)
    local_ids = jnp.clip(removed[slot_ids] - member * shard, 0, shard - 1)
    packed = jnp.take(down_rows, local_ids, axis=0)
    everyone = lax.all_gather(packed, ("row", "tp"), axis=0, tiled=True)
    lost_rows = jnp.take(everyone, owner * capacity + within, axis=0)
    cross = cross_gram.reshape(rows_local, cross_gram.shape[3])
    rhs = jnp.dot(cross, lost_rows, preferred_element_type=jnp.float32)
    leading = rhs[:half]
    stacked = lax.all_gather(leading, ("row", "tp"), axis=0, tiled=True)
    solved = jnp.dot(
        factor, stacked[:panel_width], precision=highest, preferred_element_type=jnp.float32
    )
    rhs_next = rhs - jnp.dot(left, solved, precision=highest, preferred_element_type=jnp.float32)
    return (updated.reshape(gram.shape), rhs_next.reshape(cycles, 1, half, rhs.shape[1]))


def solution(mesh):
    return jax.shard_map(
        per_device,
        mesh=mesh,
        in_specs=(
            P(None, "row", "tp", None, "col", None),
            P(),
            P(None, "row", "tp", None),
            P(("row", "tp"), "col"),
            P(),
        ),
        out_specs=(P(None, "row", "tp", None, "col", None), P(None, "row", "tp", "col")),
        check_vma=False,
    )
```

profile of v0, /device:TPU:24, one launch (start us, length us, event | category | flops | bytes accessed | tf_op | source)
XLA Modules:
  0.0 1071.5 jit_solution(9700904976470419357)
XLA Ops:
  8.0 0.0 copy-start
  8.0 0.0 all-gather.5.cloned.1.call-start
  8.1 1.5 convert_reduce_fusion.1
  9.5 0.7 fusion.10
  10.2 1.6 gather_fusion
  11.9 2.2 gather_fusion.1
  14.1 0.7 broadcast_select_fusion.1
  14.8 0.0 all-gather.5.cloned.1.call-update
  14.8 0.0 all-reduce.2.cloned.1.call-start
  14.9 3.4 broadcast_select_fusion
  18.3 1.8 copy.16
  20.1 0.0 all-reduce.2.cloned.1.call-update
  20.1 0.0 all-gather.7.cloned.1.call-start
  20.1 0.6 convert_reduce_fusion
  20.7 264.1 %all-gather.5.cloned.1.call-done = bf16[4096,512]{1,0:T(8,128)(2,1)} async-done(((bf16[128,512]{1,0:T(8,128)(2,1)}), bf16[4096,512]{1,0:T(8,128)(2,1)}) %all-gather.5.cloned.1.call-update) | async-done | bytes 4194320 | tf_op jit(solution)/shard_map/all_gather | solution.py:47
  284.8 7.8 gather_fusion.2
  292.7 2.3 convolution_bitcast_fusion
  295.0 0.7 slice.19
  295.6 0.0 all-gather.7.cloned.1.call-update
  295.7 0.2 all-gather.9.cloned.1.call-start
  295.9 0.0 all-reduce.2.cloned.1.call-done
  295.9 5.1 fusion.13
  301.0 1.3 copy-done.1
  302.3 0.7 constant_dynamic-slice_fusion
  303.1 0.0 all-gather.9.cloned.1.call-update
  303.1 6.2 copy.13
  309.3 257.5 %all-gather.7.cloned.1.call-done = f32[2048,512]{1,0:T(8,128)} async-done(((f32[64,512]{1,0:T(8,128)}), f32[2048,512]{1,0:T(8,128)}) %all-gather.7.cloned.1.call-update) | async-done | bytes 4194320 | tf_op jit(solution)/shard_map/all_gather | solution.py:52
  566.7 8.7 fusion.4
  575.4 4.5 convolution_subtract_fusion
  579.9 461.2 %all-gather.9.cloned.1.call-done = f32[1,1,2048,1024]{3,2,1,0:T(8,128)} async-done(((f32[1,1,64,1024]{3,2,1,0:T(8,128)}), f32[1,1,2048,1024]{3,2,1,0:T(8,128)}) %all-gather.9.cloned.1.call-update) | async-done | bytes 8388624 | tf_op jit(solution)/shard_map/all_gather | solution.py:31
  1041.1 16.9 %bitcast_subtract_fusion = f32[512,2048]{1,0:T(8,128)S(1)} fusion(f32[8,1,64,1,1,2048]{5,2,3,4,1,0:T(8,128)} %copy.13, f32[512,1024]{1,0:T(8,128)} %copy-done.1, f32[1,1,2048,1024]{3,2,1,0:T(8,128)} %all-gather.9.cloned.1.call-done), kind=kOutput, calls=%fused_computation.5 | convolution fusion | flops 12885950464 | bytes 18874368 | tf_op jit(solution)/shard_map/rp,cwp->rcw/dot_general | solution.py:28
  1058.0 6.3 copy.11
  (10 shorter events, 0.1 us)
Async XLA Ops:
  8.0 287.9 %copy-start = (bf16[1024,1024]{1,0:T(8,128)(2,1)S(1)}, bf16[1024,1024]{1,0:T(8,128)(2,1)}, u32[]{:S(2)}) copy-start(bf16[1024,1024]{1,0:T(8,128)(2,1)} %param.6) | copy-start | bytes 6291460
  8.0 276.8 %all-gather.5.cloned.1.call-start = ((), (), s32[]{:S(2)}) async-start(), calls=%async_computation.1 | async-start | bytes 4325376 | tf_op jit(solution)/shard_map/all_gather | solution.py:47
  14.8 281.1 %all-reduce.2.cloned.1.call-start = ((), (), s32[]{:S(2)}) async-start(), calls=%async_computation | async-start | bytes 4194304 | tf_op jit(solution)/shard_map/psum | solution.py:9
  20.1 546.6 %all-gather.7.cloned.1.call-start = ((), (), s32[]{:S(2)}) async-start(), calls=%async_computation.2 | async-start | bytes 4325376 | tf_op jit(solution)/shard_map/all_gather | solution.py:52
  295.7 745.5 %all-gather.9.cloned.1.call-start = ((), (), s32[]{:S(2)}) async-start(), calls=%async_computation.3 | async-start | bytes 8650752 | tf_op jit(solution)/shard_map/all_gather | solution.py:31
  301.0 1.3 copy-start.1
  566.7 8.7 copy-start.2
Sparse Core Ops, SparseCore 0:
  14.9 269.8 all-gather.4
  295.8 270.8 all-gather.6
  568.5 472.5 all-gather.8
Sparse Core Ops, SparseCore 1:
  20.2 75.2 all-reduce.1
where the time goes:
time: 1070 us
  waiting for transfers between devices  983 us (92%)
  matrix products  37.4 us (3%)
  local copies, waits for them, and re-layouts  28.6 us (3%)
  between operations  15.3 us (1%)
    all_gather x1, waiting for transfers between devices, per_device(): lax.all_gather(wanted, ('row', 'tp'), axis=1, tiled=True)  461 us
    all_gather x1, waiting for transfers between devices, per_device(): everyone = lax.all_gather(packed, ('row', 'tp'), axis=0, tiled=True)  264 us
    all_gather x1, waiting for transfers between devices, per_device(): stacked = lax.all_gather(leading, ('row', 'tp'), axis=0, tiled=True)  257 us
  transfers between devices with their start and end apart: 4, of which 3 were waited for; matrix products, arithmetic and copies ran while one was open for 4% of the time, Pallas kernels for 0%

commit v1 on v0

--- a/solution.py
+++ b/solution.py
@@ -49,7 +49,10 @@
     cross = cross_gram.reshape(rows_local, cross_gram.shape[3])
     rhs = jnp.dot(cross, lost_rows, preferred_element_type=jnp.float32)
     leading = rhs[:half]
-    stacked = lax.all_gather(leading, ("row", "tp"), axis=0, tiled=True)
+    stacked = jnp.concatenate(
+        lax.all_to_all(jnp.stack([leading] * lax.axis_size(("row", "tp"))), ("row", "tp"), 0, 0),
+        axis=0,
+    )
     solved = jnp.dot(
         factor, stacked[:panel_width], precision=highest, preferred_element_type=jnp.float32
     )

time: 1070 us -> 863 us (0.81)
  waiting for transfers between devices: 983 us -> 759 us
    all_gather x1 -> x0, waiting for transfers between devices: 257 us -> none  [per_device(): stacked = lax.all_gather(leading, ('row', 'tp'), axis=0, tiled=True)]
    all_to_all x0 -> x1, waiting for transfers between devices: none -> 110 us  [per_device(): lax.all_to_all(jnp.stack([leading] * lax.axis_size(('row', 'tp'))), ('row...]
    all_gather x1, waiting for transfers between devices: 461 us -> 386 us  [per_device(): lax.all_gather(wanted, ('row', 'tp'), axis=1, tiled=True)]
    all_gather x1, waiting for transfers between devices: 264 us -> 192 us  [per_device(): everyone = lax.all_gather(packed, ('row', 'tp'), axis=0, tiled=True)]
    psum x1, waiting for transfers between devices: 0.03 us -> 71 us  [broadcast(): return lax.psum(block, axis)]
  transfers between devices with their start and end apart: 4 -> 4, of which waited for: 3 -> 4; matrix products, arithmetic and copies ran while one was open for 4% -> 5% of each run, Pallas kernels for 0% -> 0%
where the time goes in v1:
time: 863 us; the launch traced here: 857 us
  waiting for transfers between devices  759 us (88%)
  matrix products  35.8 us (4%)
  local copies, waits for them, and re-layouts  30.8 us (4%)
  between operations  15.6 us (2%)
  starting transfers between devices  9.74 us (1%)
    all_gather x1, waiting for transfers between devices, per_device(): lax.all_gather(wanted, ('row', 'tp'), axis=1, tiled=True)  386 us
    all_gather x1, waiting for transfers between devices, per_device(): everyone = lax.all_gather(packed, ('row', 'tp'), axis=0, tiled=True)  192 us
    all_to_all x1, waiting for transfers between devices, per_device(): lax.all_to_all(jnp.stack([leading] * lax.axis_size(('row', 'tp'))), ('row...  110 us
    psum x1, waiting for transfers between devices, broadcast(): return lax.psum(block, axis)  71 us
  transfers between devices with their start and end apart: 4, of which 4 were waited for; matrix products, arithmetic and copies ran while one was open for 5% of the time, Pallas kernels for 0%

profile of v1, /device:TPU:24, one launch (start us, length us, event | category | flops | bytes accessed | tf_op | source)
XLA Modules:
  0.0 857.2 jit_solution(5615983317136409368)
XLA Ops:
  8.0 0.0 all-reduce.2.cloned.1.call-start
  8.1 3.5 broadcast_select_fusion
  11.6 1.8 copy.16
  13.4 0.0 all-reduce.2.cloned.1.call-update
  13.4 0.0 all-gather.4.cloned.1.call-start
  13.5 0.6 copy-done.1
  14.1 0.6 convert_reduce_fusion.1
  14.7 0.7 fusion.8
  15.4 1.0 gather_fusion
  16.4 0.8 gather_fusion.1
  17.3 0.7 broadcast_select_fusion.1
  18.0 0.0 all-gather.4.cloned.1.call-update
  18.0 0.0 all-gather.6.cloned.1.call-start
  18.1 71.0 %all-reduce.2.cloned.1.call-done = f32[512,1024]{1,0:T(8,128)} async-done(((f32[512,1024]{1,0:T(8,128)}), f32[512,1024]{1,0:T(8,128)}) %all-reduce.2.cloned.1.call-update) | async-done | bytes 2097168 | tf_op jit(solution)/shard_map/psum | solution.py:9
  89.1 5.1 fusion.11
  94.1 1.3 copy-done.2
  95.5 0.7 constant_dynamic-slice_fusion
  96.2 0.0 all-gather.6.cloned.1.call-update
  96.2 0.6 convert_reduce_fusion
  96.8 191.8 %all-gather.4.cloned.1.call-done = bf16[4096,512]{1,0:T(8,128)(2,1)} async-done(((bf16[128,512]{1,0:T(8,128)(2,1)}), bf16[4096,512]{1,0:T(8,128)(2,1)}) %all-gather.4.cloned.1.call-update) | async-done | bytes 4194320 | tf_op jit(solution)/shard_map/all_gather | solution.py:47
  288.6 7.8 gather_fusion.2
  296.5 2.3 convolution_bitcast_fusion
  298.8 2.5 stack.2
  301.3 9.6 %all-to-all-start = ((f32[32,64,512]{2,1,0:T(8,128)}), f32[32,64,512]{2,1,0:T(8,128)}, u32[]{:S(2)}, u32[]{:S(2)}) async-start(f32[32,64,512]{2,1,0:T(8,128)} %stack.2), calls=%async_computation | async-start | bytes 8388608 | tf_op jit(solution)/shard_map/all_to_all | solution.py:53
  310.9 6.2 copy.13
  317.0 109.9 %all-to-all-done = f32[32,64,512]{2,1,0:T(8,128)} async-done(((f32[32,64,512]{2,1,0:T(8,128)}), f32[32,64,512]{2,1,0:T(8,128)}, u32[]{:S(2)}, u32[]{:S(2)}) %all-to-all-start) | async-done | bytes 4194336 | tf_op jit(solution)/shard_map/all_to_all | solution.py:53
  426.9 1.8 slice.24
  428.7 6.8 fusion.12
  435.5 4.8 convolution_subtract_fusion
  440.3 386.3 %all-gather.6.cloned.1.call-done = f32[1,1,2048,1024]{3,2,1,0:T(8,128)} async-done(((f32[1,1,64,1024]{3,2,1,0:T(8,128)}), f32[1,1,2048,1024]{3,2,1,0:T(8,128)}) %all-gather.6.cloned.1.call-update) | async-done | bytes 8388624 | tf_op jit(solution)/shard_map/all_gather | solution.py:31
  826.6 16.9 %bitcast_subtract_fusion = f32[512,2048]{1,0:T(8,128)S(1)} fusion(f32[8,1,64,1,1,2048]{5,2,3,4,1,0:T(8,128)} %copy.13, f32[512,1024]{1,0:T(8,128)} %copy-done.2, f32[1,1,2048,1024]{3,2,1,0:T(8,128)} %all-gather.6.cloned.1.call-done), kind=kOutput, calls=%fused_computation.5 | convolution fusion | flops 12885950464 | bytes 18874368 | tf_op jit(solution)/shard_map/rp,cwp->rcw/dot_general | solution.py:28
  843.4 6.3 copy.11
  (15 shorter events, 0.1 us)
Async XLA Ops:
  8.0 81.1 %copy-start = (bf16[1024,1024]{1,0:T(8,128)(2,1)S(1)}, bf16[1024,1024]{1,0:T(8,128)(2,1)}, u32[]{:S(2)}) copy-start(bf16[1024,1024]{1,0:T(8,128)(2,1)} %param.6) | copy-start | bytes 6291460
  8.0 81.1 %all-reduce.2.cloned.1.call-start = ((), (), s32[]{:S(2)}) async-start(), calls=%async_computation.1 | async-start | bytes 4194304 | tf_op jit(solution)/shard_map/psum | solution.py:9
  13.4 0.7 copy-start.1
  13.4 3.0 copy-start.4
  13.4 275.2 %all-gather.4.cloned.1.call-start = ((), (), s32[]{:S(2)}) async-start(), calls=%async_computation.2 | async-start | bytes 4325376 | tf_op jit(solution)/shard_map/all_gather | solution.py:47
  18.0 808.5 %all-gather.6.cloned.1.call-start = ((), (), s32[]{:S(2)}) async-start(), calls=%async_computation.3 | async-start | bytes 8650752 | tf_op jit(solution)/shard_map/all_gather | solution.py:31
  94.1 1.3 copy-start.2
  301.3 125.7 %all-to-all-start = ((f32[32,64,512]{2,1,0:T(8,128)}), f32[32,64,512]{2,1,0:T(8,128)}, u32[]{:S(2)}, u32[]{:S(2)}) async-start(f32[32,64,512]{2,1,0:T(8,128)} %stack.2), calls=%async_computation | async-start | bytes 8388608 | tf_op jit(solution)/shard_map/all_to_all | solution.py:53
  428.7 6.9 copy-start.3
Sparse Core Ops, SparseCore 0:
  13.5 75.4 all-reduce.1
Sparse Core Ops, SparseCore 1:
  18.1 270.4 all-gather.3
  290.3 536.2 all-gather.5
